TPU v7x, 32 devices: a whole 2x2x4 slice. The times are simulated.
32 devices in a mesh: rep: 4 (over x, core), space: 8 (over z, y).
Axes of the slice: x: 2, y: 2, z: 4, core: 2. Of those that a mesh axis runs over, the one named last changes fastest.
Arguments:
- phase_space: float32 [4, 6, 4, 16384], P('rep', None, None, 'space'), may hold values from -6 to 6
- charges: float32 [4, 4, 16384], P('rep', None, 'space'), may hold values from -4 to 4
- lj_depth: float32 [4, 4, 16384], P('rep', None, 'space'), may hold values from 0.5 to 2
- cluster_fill: int32 [4, 16384], P('rep', 'space'), may hold values from 1 to 4
- neighbours: int32 [4, 16, 16384], P('rep', None, 'space'), may hold values from 0 to 3071
- ghost_send: int32 [4, 8192], P('rep', 'space'), may hold values from 0 to 2047
- partner: int32 [4], replicated, may hold values from 0 to 3, as said below
- scale_order: int32 [4], replicated, may hold values from 0 to 3, as said below
- coupling: float32 [4], replicated, may hold values from 0.25 to 1
Outputs:
- advanced: float32 [4, 6, 4, 16384], P('rep', None, None, 'space')
Inputs may be any that keep to these rules, and one draw needn't show every extreme that they name: partner[l] is l - 1, l or l + 1, and partner[partner[l]] = l; for one p of 0 or 1, the same for the whole matching, every swapped pair is (2k + p, 2k + p + 1). `scale_order`: each level once.
All inputs are finite; a program needn't handle non-finite values.
Results may differ from a plain program's by a relative error of at most 0.0003.
Values sent between devices are 32-bit elements; how exact they have to be, the bound alone decides.
A program may use at most 128 MiB of HBM per device.

v0:
```python
import jax
import jax.numpy as jnp
from jax import lax
from jax.sharding import PartitionSpec as P

STEPS = 2


time_step = 0.2
softening = 0.5


def padded_2(block, sides, width):
    for axis, dim in sides:
        count = lax.axis_size(axis)
        forward = [(i, i + 1) for i in range(count - 1)]
        forward.append((count - 1, 0))
        backward = [(target, source) for source, target in forward]
        low = lax.ppermute(
            lax.slice_in_dim(block, block.shape[dim] - width, None, axis=dim), axis, forward
        )
        high = lax.ppermute(lax.slice_in_dim(block, 0, width, axis=dim), axis, backward)
        block = jnp.concatenate([low, block, high], axis=dim)
    return block


def cluster_forces(positions, params, pool_pos, pool_par, near_list, strength):
    total = positions.shape[2]
    block_size = min(512, total)
    block_count = total // block_size

    def block_forces(block_id):
        first_row = block_id * block_size
        own_pos = lax.dynamic_slice_in_dim(positions, first_row, block_size, 2)
        own_par = lax.dynamic_slice_in_dim(params, first_row, block_size, 2)
        slot_ids = lax.dynamic_slice_in_dim(near_list, first_row, block_size, 1)
        other_pos = pool_pos[:, :, slot_ids]
        other_par = pool_par[:, :, slot_ids]
        offset = own_pos[:, :, None, None, :] - other_pos[:, None]
        inverse = 1.0 / (jnp.sum(offset * offset, axis=0) + softening)
        charge_pair = own_par[0][:, None, None, :] * other_par[0][None]
        depth_pair = own_par[1][:, None, None, :] * other_par[1][None]
        weight = strength * charge_pair * inverse * jnp.sqrt(inverse) + depth_pair * (
            inverse**3 - inverse**2
        )
        return jnp.sum(weight[None] * offset, axis=(2, 3))

    stacked = lax.map(block_forces, jnp.arange(block_count, dtype=jnp.int32))
    return jnp.moveaxis(stacked, 0, 2).reshape(3, positions.shape[1], total)


def edge_ghosts(padded, ghost_width):
    return jnp.concatenate([padded[:, :, :ghost_width], padded[:, :, 3 * ghost_width :]], 2)


def on_device(
    phase_space,
    charges,
    lj_depth,
    cluster_fill,
    neighbours,
    ghost_send,
    partner,
    scale_order,
    coupling,
):
    phase_now = phase_space[0]
    my_index = lax.axis_index("rep")
    replica_count = lax.axis_size("rep")
    piece_width = phase_now.shape[2] // replica_count
    pieces = phase_now.reshape(phase_now.shape[0], phase_now.shape[1], replica_count, piece_width)
    pieces_in = lax.all_to_all(pieces, "rep", split_axis=2, concat_axis=2, tiled=True)
    picked = jnp.take(pieces_in, partner, axis=2)
    returned = lax.all_to_all(picked, "rep", split_axis=2, concat_axis=2, tiled=True)
    phase_now = returned.reshape(phase_now.shape)
    strength = coupling[scale_order[my_index]]
    atom_slot = jnp.arange(phase_now.shape[1], dtype=jnp.int32)[:, None]
    present = (atom_slot < cluster_fill[0][None, :]).astype(jnp.float32)
    params = jnp.stack([charges[0] * present, lj_depth[0] * present])
    senders = ghost_send[0]
    ghost_width = senders.shape[0] // 2
    near_list = neighbours[0]
    positions = phase_now[:3]
    velocity = phase_now[3:]
    ghost_params = params[:, :, :0]
    for step_index in range(STEPS):
        packet = jnp.concatenate([positions, params], 0)[:, :, senders]
        padded = padded_2(packet, (("space", 2),), ghost_width)
        ghosts = edge_ghosts(padded, ghost_width)
        ghost_pos = ghosts[:3]
        ghost_params = ghosts[3:]
        pool_pos = jnp.concatenate([positions, ghost_pos], 2)
        pool_par = jnp.concatenate([params, ghost_params], 2)
        forces = cluster_forces(positions, params, pool_pos, pool_par, near_list, strength)
        velocity = velocity + time_step * forces
        positions = positions + time_step * velocity
    return jnp.concatenate([positions, velocity], 0)[None]


def solution(mesh):
    return jax.shard_map(
        on_device,
        mesh=mesh,
        in_specs=(
            P("rep", None, None, "space"),
            P("rep", None, "space"),
            P("rep", None, "space"),
            P("rep", "space"),
            P("rep", None, "space"),
            P("rep", "space"),
            P(),
            P(),
            P(),
        ),
        out_specs=P("rep", None, None, "space"),
        check_vma=False,
    )
```

profile of v0, /device:TPU:0, one launch (start us, length us, event | category | flops | bytes accessed | tf_op | source)
XLA Modules:
  0.0 1290.7 jit_solution(5801446564905513694)
XLA Ops:
  1.8 4.2 all-to-all-start
  8.9 2.5 all-to-all-done
  12.9 3.4 all-to-all-start.1
  16.2 5.3 all-to-all-done.1
  21.6 3.1 copy.105
  24.7 10.1 gather_fusion.5
  42.6 3.1 collective-permute-start.1
  47.5 3.4 copy.108
  51.0 4.5 copy.109
  55.5 601.6 %while.20 = (s32[]{:T(128)}, f32[4,3,4,512]{3,2,1,0:T(4,128)S(1)}, f32[]{:T(128)}, s32[4]{0:T(128)S(1)}, f32[2,4,2048]{2,1,0:T(4,128)S(1)}, /*index=5*/s32[16,20...) while((s32[]{:T(128)}, f32[4,3,4,512]{3,2,1,0:T(4,128)S(1)}, ...), condition=%wide.region_3.4_spmd, body=%wide.region_0.3_spmd.sunk | while | flops 3827719 | bytes 6775019 | solution.py:48
  56.9 58.4 %gather_fusion.1 = f32[8192,2,4]{2,1,0:T(2,128)} fusion(f32[2,4,3072]{1,0,2:T(2,128)} %get-tuple-element.401, s32[8192]{0:T(1024)S(1)} %broadcast_clamp_fusion.5), kind=kCustom, calls=%fused_computation.clone.1 | custom fusion | bytes 557056 | tf_op jit(solution)/shard_map/while/body/eval_jaxpr/gather | solution.py:38
  115.3 11.6 fusion.29
  126.9 2.9 copy.132
  129.7 2.9 copy.133
  132.6 62.5 %gather_fusion = f32[8192,3,4]{2,1,0:T(4,128)} fusion(f32[3,4,3072]{1,0,2:T(4,128)} %get-tuple-element.403, s32[8192]{0:T(1024)S(1)} %broadcast_clamp_fusion.5), kind=kCustom, calls=%fused_computation.1.clone.1 | custom fusion | bytes 819200 | tf_op jit(solution)/shard_map/while/body/eval_jaxpr/gather | solution.py:37
  195.1 9.4 copy.131
  207.3 58.4 %gather_fusion.1 = f32[8192,2,4]{2,1,0:T(2,128)} fusion(f32[2,4,3072]{1,0,2:T(2,128)} %get-tuple-element.401, s32[8192]{0:T(1024)S(1)} %broadcast_clamp_fusion.5), kind=kCustom, calls=%fused_computation.clone.1 | custom fusion | bytes 557056 | tf_op jit(solution)/shard_map/while/body/eval_jaxpr/gather | solution.py:38
  265.7 11.6 fusion.29
  277.3 2.9 copy.132
  280.1 2.9 copy.133
  283.0 62.5 %gather_fusion = f32[8192,3,4]{2,1,0:T(4,128)} fusion(f32[3,4,3072]{1,0,2:T(4,128)} %get-tuple-element.403, s32[8192]{0:T(1024)S(1)} %broadcast_clamp_fusion.5), kind=kCustom, calls=%fused_computation.1.clone.1 | custom fusion | bytes 819200 | tf_op jit(solution)/shard_map/while/body/eval_jaxpr/gather | solution.py:37
  345.5 9.4 copy.131
  357.7 58.4 %gather_fusion.1 = f32[8192,2,4]{2,1,0:T(2,128)} fusion(f32[2,4,3072]{1,0,2:T(2,128)} %get-tuple-element.401, s32[8192]{0:T(1024)S(1)} %broadcast_clamp_fusion.5), kind=kCustom, calls=%fused_computation.clone.1 | custom fusion | bytes 557056 | tf_op jit(solution)/shard_map/while/body/eval_jaxpr/gather | solution.py:38
  416.1 11.6 fusion.29
  427.7 2.9 copy.132
  430.5 2.9 copy.133
  433.4 62.5 %gather_fusion = f32[8192,3,4]{2,1,0:T(4,128)} fusion(f32[3,4,3072]{1,0,2:T(4,128)} %get-tuple-element.403, s32[8192]{0:T(1024)S(1)} %broadcast_clamp_fusion.5), kind=kCustom, calls=%fused_computation.1.clone.1 | custom fusion | bytes 819200 | tf_op jit(solution)/shard_map/while/body/eval_jaxpr/gather | solution.py:37
  495.9 9.4 copy.131
  508.1 58.4 %gather_fusion.1 = f32[8192,2,4]{2,1,0:T(2,128)} fusion(f32[2,4,3072]{1,0,2:T(2,128)} %get-tuple-element.401, s32[8192]{0:T(1024)S(1)} %broadcast_clamp_fusion.5), kind=kCustom, calls=%fused_computation.clone.1 | custom fusion | bytes 557056 | tf_op jit(solution)/shard_map/while/body/eval_jaxpr/gather | solution.py:38
  566.4 11.6 fusion.29
  578.0 2.9 copy.132
  580.9 2.9 copy.133
  583.8 62.5 %gather_fusion = f32[8192,3,4]{2,1,0:T(4,128)} fusion(f32[3,4,3072]{1,0,2:T(4,128)} %get-tuple-element.403, s32[8192]{0:T(1024)S(1)} %broadcast_clamp_fusion.5), kind=kCustom, calls=%fused_computation.1.clone.1 | custom fusion | bytes 819200 | tf_op jit(solution)/shard_map/while/body/eval_jaxpr/gather | solution.py:37
  646.3 9.4 copy.131
  657.3 3.1 copy.111
  660.4 10.1 gather_fusion.6
  674.7 3.4 collective-permute-start.3
  679.9 3.4 copy.114
  683.3 4.5 copy.115
  687.9 602.0 %while.21 = (s32[]{:T(128)}, f32[4,3,4,512]{3,2,1,0:T(4,128)S(1)}, f32[]{:T(128)}, s32[4]{0:T(128)S(1)}, f32[2,4,2048]{2,1,0:T(4,128)S(1)}, /*index=5*/s32[16,20...) while((s32[]{:T(128)}, f32[4,3,4,512]{3,2,1,0:T(4,128)S(1)}, ...), condition=%wide.region_7.8_spmd, body=%wide.region_4.7_spmd.sunk | while | flops 3827719 | bytes 6775019 | solution.py:48
  689.3 58.4 %gather_fusion.3 = f32[8192,2,4]{2,1,0:T(2,128)} fusion(f32[2,4,3072]{1,0,2:T(2,128)} %get-tuple-element.443, s32[8192]{0:T(1024)S(1)} %broadcast_clamp_fusion.6), kind=kCustom, calls=%fused_computation.2.clone.1 | custom fusion | bytes 557056 | tf_op jit(solution)/shard_map/while/body/eval_jaxpr/gather | solution.py:38
  747.7 11.6 fusion.34
  759.3 2.9 copy.136
  762.1 2.9 copy.137
  765.0 62.5 %gather_fusion.2 = f32[8192,3,4]{2,1,0:T(4,128)} fusion(f32[3,4,3072]{1,0,2:T(4,128)} %get-tuple-element.445, s32[8192]{0:T(1024)S(1)} %broadcast_clamp_fusion.6), kind=kCustom, calls=%fused_computation.3.clone.1 | custom fusion | bytes 819200 | tf_op jit(solution)/shard_map/while/body/eval_jaxpr/gather | solution.py:37
  827.5 9.4 copy.135
  839.8 58.4 %gather_fusion.3 = f32[8192,2,4]{2,1,0:T(2,128)} fusion(f32[2,4,3072]{1,0,2:T(2,128)} %get-tuple-element.443, s32[8192]{0:T(1024)S(1)} %broadcast_clamp_fusion.6), kind=kCustom, calls=%fused_computation.2.clone.1 | custom fusion | bytes 557056 | tf_op jit(solution)/shard_map/while/body/eval_jaxpr/gather | solution.py:38
  898.2 11.6 fusion.34
  909.8 2.9 copy.136
  912.6 2.9 copy.137
  915.5 62.5 %gather_fusion.2 = f32[8192,3,4]{2,1,0:T(4,128)} fusion(f32[3,4,3072]{1,0,2:T(4,128)} %get-tuple-element.445, s32[8192]{0:T(1024)S(1)} %broadcast_clamp_fusion.6), kind=kCustom, calls=%fused_computation.3.clone.1 | custom fusion | bytes 819200 | tf_op jit(solution)/shard_map/while/body/eval_jaxpr/gather | solution.py:37
  978.0 9.4 copy.135
  990.3 58.4 %gather_fusion.3 = f32[8192,2,4]{2,1,0:T(2,128)} fusion(f32[2,4,3072]{1,0,2:T(2,128)} %get-tuple-element.443, s32[8192]{0:T(1024)S(1)} %broadcast_clamp_fusion.6), kind=kCustom, calls=%fused_computation.2.clone.1 | custom fusion | bytes 557056 | tf_op jit(solution)/shard_map/while/body/eval_jaxpr/gather | solution.py:38
  1048.7 11.6 fusion.34
  1060.3 2.9 copy.136
  1063.1 2.9 copy.137
  1066.0 62.5 %gather_fusion.2 = f32[8192,3,4]{2,1,0:T(4,128)} fusion(f32[3,4,3072]{1,0,2:T(4,128)} %get-tuple-element.445, s32[8192]{0:T(1024)S(1)} %broadcast_clamp_fusion.6), kind=kCustom, calls=%fused_computation.3.clone.1 | custom fusion | bytes 819200 | tf_op jit(solution)/shard_map/while/body/eval_jaxpr/gather | solution.py:37
  1128.5 9.4 copy.135
  1140.8 58.4 %gather_fusion.3 = f32[8192,2,4]{2,1,0:T(2,128)} fusion(f32[2,4,3072]{1,0,2:T(2,128)} %get-tuple-element.443, s32[8192]{0:T(1024)S(1)} %broadcast_clamp_fusion.6), kind=kCustom, calls=%fused_computation.2.clone.1 | custom fusion | bytes 557056 | tf_op jit(solution)/shard_map/while/body/eval_jaxpr/gather | solution.py:38
  1199.2 11.6 fusion.34
  1210.8 2.9 copy.136
  1213.6 2.9 copy.137
  1216.5 62.5 %gather_fusion.2 = f32[8192,3,4]{2,1,0:T(4,128)} fusion(f32[3,4,3072]{1,0,2:T(4,128)} %get-tuple-element.445, s32[8192]{0:T(1024)S(1)} %broadcast_clamp_fusion.6), kind=kCustom, calls=%fused_computation.3.clone.1 | custom fusion | bytes 819200 | tf_op jit(solution)/shard_map/while/body/eval_jaxpr/gather | solution.py:37
  1279.0 9.4 copy.135
  (139 shorter events, 37.5 us)
Async XLA Ops:
  1.8 9.5 all-to-all-start
  12.9 8.6 all-to-all-start.1
  21.6 17.5 %copy-start.1 = (s32[4]{0:T(128)S(1)}, s32[4]{0:T(128)}, u32[]{:S(2)}) copy-start(s32[4]{0:T(128)} %param.20) | copy-start | bytes 52
  21.6 20.0 %copy-start.2 = (f32[4]{0:T(128)S(1)}, f32[4]{0:T(128)}, u32[]{:S(2)}) copy-start(f32[4]{0:T(128)} %param.21) | copy-start | bytes 52
  36.9 8.8 collective-permute-start
  42.6 4.8 collective-permute-start.1
  47.5 8.0 copy-start
  672.6 7.1 collective-permute-start.2
  674.7 5.0 collective-permute-start.3
where the time goes:
time: 1290 us
  local copies, waits for them, and re-layouts  1240 us (96%)
  starting transfers between devices  18 us (1%)
  other arithmetic  16.2 us (1%)
    gather x16, local copies, waits for them, and re-layouts, block_forces(): other_pos = pool_pos[:, :, slot_ids]  575 us
    gather x8, local copies, waits for them, and re-layouts, block_forces(): other_par = pool_par[:, :, slot_ids]  467 us
    slice x8, local copies, waits for them, and re-layouts, block_forces(): charge_pair = own_par[0][:, None, None, :] * other_par[0][None]  92.8 us
  transfers between devices with their start and end apart: 6, of which 5 were waited for; matrix products, arithmetic and copies ran while one was open for 0% of the time, Pallas kernels for 0%

commit v1 on v0

v1 whole, which is shorter than its diff:
```python
import functools

import jax
import jax.numpy as jnp
from jax import lax
from jax.experimental import pallas as pl
from jax.experimental.pallas import tpu as pltpu
from jax.sharding import PartitionSpec as P

STEPS = 2
LANES = 128

time_step = 0.2
softening = 0.5

VMEM = pl.BlockSpec(memory_space=pltpu.VMEM)
SMEM = pl.BlockSpec(memory_space=pltpu.SMEM)
f32 = jnp.float32


def upper_half():
    return lax.broadcasted_iota(jnp.int32, (8, LANES), 0) >= 4


def row(values):
    return jnp.broadcast_to(values, (8, LANES))


def fill_table(tab, c, first, block):
    for k in range(block.shape[1] // LANES):
        tile = block[:, k * LANES : (k + 1) * LANES]
        tab[c, first + k] = jnp.concatenate([tile, tile], 0)


def lookup(tab, comps, tiles, index):
    low = index & (LANES - 1)
    high = index >> 7
    found = [None] * len(comps)
    for k in range(tiles):
        mask = high == k
        for n, c in enumerate(comps):
            got = jnp.take_along_axis(tab[c, k], low, axis=1)
            found[n] = got if k == 0 else jnp.where(mask, got, found[n])
    return found


def send_ghosts(tab, comps, tiles, gs, out_first, out_last):
    width = out_first.shape[2]
    up = upper_half()
    for g in range(width // LANES):
        index = jnp.where(
            up,
            row(gs[:, width + g * LANES : width + (g + 1) * LANES]),
            row(gs[:, g * LANES : (g + 1) * LANES]),
        )
        for c, got in zip(range(comps), lookup(tab, range(comps), tiles, index)):
            out_first[c, :, g * LANES : (g + 1) * LANES] = got[:4]
            out_last[c, :, g * LANES : (g + 1) * LANES] = got[4:]


def params_kernel(charges, lj, fill, gs, par, out_first, out_last, tab):
    total = charges.shape[1]
    slot = lax.broadcasted_iota(jnp.int32, (4, total), 0)
    present = (slot < fill[...]).astype(f32)
    par[0] = charges[...] * present
    par[1] = lj[...] * present
    for c in range(2):
        fill_table(tab, c, 0, par[c])
    send_ghosts(tab, 2, total // LANES, gs, out_first, out_last)


def swap_kernel(sel, mine, low, high, gs, pos, out_first, out_last, tab):
    total = mine.shape[2]
    which = sel[0]
    for c in range(3):
        block = jnp.where(which == 0, mine[c], jnp.where(which < 0, low[c], high[c]))
        pos[c] = block
        fill_table(tab, c, 0, block)
    send_ghosts(tab, 3, total // LANES, gs, out_first, out_last)


def pair_index(near, pair, base):
    return jnp.where(
        upper_half(),
        row(near[2 * pair + 1 : 2 * pair + 2, pl.ds(base, LANES)]),
        row(near[2 * pair : 2 * pair + 1, pl.ds(base, LANES)]),
    )


def gather_kernel(par, from_low, from_high, near, out, tab):
    total, width = par.shape[2], from_low.shape[2]
    own, ghost = total // LANES, width // LANES
    for c in range(2):
        fill_table(tab, c, 0, par[c])
        fill_table(tab, c, own, from_low[c])
        fill_table(tab, c, own + ghost, from_high[c])
    tiles = own + 2 * ghost

    def body(group, carry):
        base = pl.multiple_of(group * LANES, LANES)
        for pair in range(near.shape[0] // 2):
            got = lookup(tab, (0, 1), tiles, pair_index(near, pair, base))
            out[group, pair, 0] = got[0]
            out[group, pair, 1] = got[1]
        return carry

    lax.fori_loop(0, own, body, 0)


def step_body(strength, pos, from_low, from_high, par, gathered, near, velocity, new_pos, new_vel, tab):
    total, width = pos.shape[2], from_low.shape[2]
    own, ghost = total // LANES, width // LANES
    for c in range(3):
        fill_table(tab, c, 0, pos[c])
        fill_table(tab, c, own, from_low[c])
        fill_table(tab, c, own + ghost, from_high[c])
    tiles = own + 2 * ghost
    scale = strength[0]

    def body(group, carry):
        base = pl.multiple_of(group * LANES, LANES)
        lanes = pl.ds(base, LANES)
        force = [[None] * 4 for _ in range(3)]
        for pair in range(near.shape[0] // 2):
            there = lookup(tab, (0, 1, 2), tiles, pair_index(near, pair, base))
            charge = gathered[group, pair, 0] * scale
            depth = gathered[group, pair, 1]
            for i in range(4):
                offset = [row(pos[c, i : i + 1, lanes]) - there[c] for c in range(3)]
                square = offset[0] * offset[0] + offset[1] * offset[1] + offset[2] * offset[2]
                root = lax.rsqrt(square + softening)
                w = root * root
                qq = row(par[0, i : i + 1, lanes]) * charge
                ee = row(par[1, i : i + 1, lanes]) * depth
                weight = w * (qq * root + ee * (w * w - w))
                for c in range(3):
                    term = weight * offset[c]
                    force[c][i] = term if pair == 0 else force[c][i] + term
        for c in range(3):
            rows = [jnp.sum(force[c][i], axis=0, keepdims=True) for i in range(4)]
            v = velocity(c, lanes) + time_step * jnp.concatenate(rows, 0)
            new_vel(c, lanes, v)
            new_pos(c, lanes, pos[c, :, lanes] + time_step * v)
        return carry

    lax.fori_loop(0, own, body, 0)


def first_step_kernel(
    sel, strength, pos, from_low, from_high, par, gathered, near, mine, low, high, gs,
    pos_out, vel_out, out_first, out_last, tab,
):
    which = sel[0]

    def velocity(c, lanes):
        return jnp.where(
            which == 0, mine[c, :, lanes],
            jnp.where(which < 0, low[c, :, lanes], high[c, :, lanes]),
        )

    def new_vel(c, lanes, v):
        vel_out[c, :, lanes] = v

    def new_pos(c, lanes, v):
        pos_out[c, :, lanes] = v

    step_body(strength, pos, from_low, from_high, par, gathered, near, velocity, new_pos, new_vel, tab)
    total = pos.shape[2]
    for c in range(3):
        fill_table(tab, c, 0, pos_out[c])
    send_ghosts(tab, 3, total // LANES, gs, out_first, out_last)


def last_step_kernel(
    strength, pos, from_low, from_high, par, gathered, near, vel, out, tab
):
    def velocity(c, lanes):
        return vel[c, :, lanes]

    def new_vel(c, lanes, v):
        out[3 + c, :, lanes] = v

    def new_pos(c, lanes, v):
        out[c, :, lanes] = v

    step_body(strength, pos, from_low, from_high, par, gathered, near, velocity, new_pos, new_vel, tab)


def call(kernel, outs, args, smem, comps, tiles, flops=0):
    return pl.pallas_call(
        kernel,
        out_shape=[jax.ShapeDtypeStruct(s, f32) for s in outs],
        in_specs=[SMEM] * smem + [VMEM] * (len(args) - smem),
        out_specs=[VMEM] * len(outs),
        scratch_shapes=[pltpu.VMEM((comps, tiles, 8, LANES), f32)],
        cost_estimate=pl.CostEstimate(flops=flops, bytes_accessed=1 << 20, transcendentals=0),
    )(*args)


def on_device(
    phase_space, charges, lj_depth, cluster_fill, neighbours, ghost_send, partner, scale_order, coupling
):
    phase = phase_space[0]
    slots, total = phase.shape[1:]
    width = ghost_send.shape[1] // 2
    near = neighbours[0]
    level, levels = lax.axis_index("rep"), lax.axis_size("rep")
    spaces = lax.axis_size("space")
    up = [(i, i + 1) for i in range(levels - 1)]
    down = [(i + 1, i) for i in range(levels - 1)]
    ring_up = [(i, (i + 1) % spaces) for i in range(spaces)]
    ring_down = [(b, a) for a, b in ring_up]

    def to_neighbours(first, last):
        return lax.ppermute(last, "space", ring_up), lax.ppermute(first, "space", ring_down)

    mine_pos, mine_vel = phase[:3], phase[3:]
    pos_low, pos_high = lax.ppermute(mine_pos, "rep", up), lax.ppermute(mine_pos, "rep", down)
    vel_low, vel_high = lax.ppermute(mine_vel, "rep", up), lax.ppermute(mine_vel, "rep", down)
    sel = (partner[level] - level).astype(jnp.int32).reshape(1)
    strength = coupling[scale_order[level]].reshape(1)

    own = total // LANES
    tiles = own + 2 * (width // LANES)
    ghosts = lambda comps: [(comps, slots, width)] * 2
    pairs = near.shape[0] // 2

    par, first, last = call(
        params_kernel, [(2, slots, total)] + ghosts(2),
        (charges[0], lj_depth[0], cluster_fill, ghost_send), 0, 2, own,
    )
    par_low, par_high = to_neighbours(first, last)
    pos, first, last = call(
        swap_kernel, [(3, slots, total)] + ghosts(3),
        (sel, mine_pos, pos_low, pos_high, ghost_send), 1, 3, own,
    )
    ghost_low, ghost_high = to_neighbours(first, last)
    (gathered,) = call(
        gather_kernel, [(own, pairs, 2, 8, LANES)], (par, par_low, par_high, near), 0, 2, tiles, 1 << 24
    )
    pos, vel, first, last = call(
        first_step_kernel, [(3, slots, total)] * 2 + ghosts(3),
        (sel, strength, pos, ghost_low, ghost_high, par, gathered, near, mine_vel, vel_low, vel_high, ghost_send),
        2, 3, tiles, 1 << 25,
    )
    ghost_low, ghost_high = to_neighbours(first, last)
    (out,) = call(
        last_step_kernel, [(6, slots, total)],
        (strength, pos, ghost_low, ghost_high, par, gathered, near, vel), 1, 3, tiles, 1 << 25,
    )
    return out[None]


def solution(mesh):
    return jax.shard_map(
        on_device,
        mesh=mesh,
        in_specs=(
            P("rep", None, None, "space"),
            P("rep", None, "space"),
            P("rep", None, "space"),
            P("rep", "space"),
            P("rep", None, "space"),
            P("rep", "space"),
            P(),
            P(),
            P(),
        ),
        out_specs=P("rep", None, None, "space"),
        check_vma=False,
    )
```

time: 1290 us -> 76.7 us (0.06)
  local copies, waits for them, and re-layouts: 1240 us -> 5.95 us
  Pallas kernels: 0 us -> 43.2 us
  other arithmetic: 16.2 us -> 0 us
    gather x27 -> x0, local copies, waits for them, and re-layouts: 1060 us -> none  [the longest x16 575 us: block_forces(): other_pos = pool_pos[:, :, slot_ids]]
    slice x19 -> x1, local copies, waits for them, and re-layouts: 97.6 us -> 0.95 us  [on_device(): mine_pos, mine_vel = (phase[:3], phase[3:])]
    mul x25 -> x0, local copies, waits for them, and re-layouts: 45.8 us -> none  [the longest x16 22.9 us: block_forces(): charge_pair = own_par[0][:, None, None, :] * other_par[0][None]]
    pallas_call x0 -> x5, Pallas kernels: none -> 43.2 us  [call(): pl.pallas_call(kernel, out_shape=[jax.ShapeDtypeStruct(s, f32) for s in o...]
    while x12 -> x0, local copies, waits for them, and re-layouts: 16 us -> none  [the longest x4 15.9 us: cluster_forces(): stacked = lax.map(block_forces, jnp.arange(block_count, dtype=jnp.int32))]
  transfers between devices with their start and end apart: 6 -> 10, of which waited for: 5 -> 2; matrix products, arithmetic and copies ran while one was open for 0% -> 2% of each run, Pallas kernels for 0% -> 18%
where the time goes in v1:
time: 76.7 us; the launch traced here: 76.3 us
  Pallas kernels  43.2 us (56%)
  starting transfers between devices  22.3 us (29%)
  local copies, waits for them, and re-layouts  5.95 us (8%)
  between operations  2.65 us (3%)
  waiting for transfers between devices  2.22 us (3%)
    pallas_call x5, Pallas kernels, call(): pl.pallas_call(kernel, out_shape=[jax.ShapeDtypeStruct(s, f32) for s in o...  43.2 us
    ppermute x3, starting transfers between devices, to_neighbours(): lax.ppermute(first, 'space', ring_down)  7.15 us
    ppermute x1, starting transfers between devices, on_device(): lax.ppermute(mine_vel, 'rep', up)  5.12 us
    ppermute x3, starting transfers between devices, to_neighbours(): lax.ppermute(last, 'space', ring_up)  4.37 us
    unnamed x32, local copies, waits for them, and re-layouts  3.17 us
    ppermute x1, starting transfers between devices, on_device(): lax.ppermute(mine_pos, 'rep', up)  3.04 us
    ppermute x3, waiting for transfers between devices, to_neighbours(): lax.ppermute(last, 'space', ring_up)  2.02 us
  transfers between devices with their start and end apart: 10, of which 2 were waited for; matrix products, arithmetic and copies ran while one was open for 2% of the time, Pallas kernels for 18%

profile of v1, /device:TPU:0, one launch (start us, length us, event | category | flops | bytes accessed | tf_op | source)
XLA Modules:
  0.0 76.3 jit_solution(3605871560270226109)
XLA Ops:
  0.0 1.0 %slice_bitcast_fusion = (f32[3,4,2048]{2,1,0:T(4,128)S(1)}, f32[3,4,2048]{2,1,0:T(4,128)S(1)}) fusion(f32[1,6,4,2048]{3,2,1,0:T(4,128)} %param.9), kind=kLoop, calls=%fused_computation | loop fusion | bytes 393216 | tf_op jit(solution)/shard_map/slice | solution.py:217
  1.0 0.0 copy-start.1
  1.0 0.0 copy-start
  1.0 1.3 %collective-permute-start.1 = (f32[3,4,2048]{2,1,0:T(4,128)S(1)}, f32[3,4,2048]{2,1,0:T(4,128)S(1)}, u32[]{:S(2)}, u32[]{:S(2)}) collective-permute-start(f32[3,4,2048]{2,1,0:T(4,128)S(1)} %get-tuple-element.26.mine), channel_id=1, source_target_pairs={{8,0},{16,8},{24,16},{9,1},{17,9},{25,17},{10,2},{18,10},{26,18},{... | collective-permute-start | bytes 294920 | tf_op jit(solution)/shard_map/ppermute | solution.py:218
  2.3 3.0 %collective-permute-start = (f32[3,4,2048]{2,1,0:T(4,128)S(1)}, f32[3,4,2048]{2,1,0:T(4,128)S(1)}, u32[]{:S(2)}, u32[]{:S(2)}) collective-permute-start(f32[3,4,2048]{2,1,0:T(4,128)S(1)} %get-tuple-element.26.mine), channel_id=1, source_target_pairs={{0,8},{8,16},{16,24},{1,9},{9,17},{17,25},{2,10},{10,18},{18,26},{... | collective-permute-start | bytes 294920 | tf_op jit(solution)/shard_map/ppermute | solution.py:218
  5.3 1.3 %collective-permute-start.7 = (f32[3,4,2048]{2,1,0:T(4,128)S(1)}, f32[3,4,2048]{2,1,0:T(4,128)S(1)}, u32[]{:S(2)}, u32[]{:S(2)}) collective-permute-start(f32[3,4,2048]{2,1,0:T(4,128)S(1)} %get-tuple-element.25.mine), channel_id=1, source_target_pairs={{8,0},{16,8},{24,16},{9,1},{17,9},{25,17},{10,2},{18,10},{26,18},{... | collective-permute-start | bytes 294920 | tf_op jit(solution)/shard_map/ppermute | solution.py:219
  6.6 5.1 %collective-permute-start.6 = (f32[3,4,2048]{2,1,0:T(4,128)S(1)}, f32[3,4,2048]{2,1,0:T(4,128)S(1)}, u32[]{:S(2)}, u32[]{:S(2)}) collective-permute-start(f32[3,4,2048]{2,1,0:T(4,128)S(1)} %get-tuple-element.25.mine), channel_id=1, source_target_pairs={{0,8},{8,16},{16,24},{1,9},{9,17},{17,25},{2,10},{10,18},{18,26},{... | collective-permute-start | bytes 294920 | tf_op jit(solution)/shard_map/ppermute | solution.py:219
  11.8 1.6 %shard_map.92 = (f32[2,4,2048]{2,1,0:T(4,128)}, f32[2,4,512]{2,1,0:T(4,128)}, f32[2,4,512]{2,1,0:T(4,128)}) custom-call(f32[4,2048]{1,0:T(4,128)} %bitcast.14, f32[4,2048]{1,0:T(4,128)} %bitcast.15, s32[1,2048]{1,0:T(1,128)} %fill.1, s32[1,1024]{1,0:T(1,128)} %gs.5), custom_call_target="tpu_custom_call" | custom-call | bytes 1048576 | tf_op jit(solution)/shard_map/pallas_call | solution.py:190
  13.4 1.5 %collective-permute-start.4 = (f32[2,4,512]{2,1,0:T(4,128)}, f32[2,4,512]{2,1,0:T(4,128)S(1)}, u32[]{:S(2)}, u32[]{:S(2)}) collective-permute-start(f32[2,4,512]{2,1,0:T(4,128)} %get-tuple-element.19), channel_id=1, source_target_pairs={{0,1},{1,2},{2,3},{3,4},{4,5},{5,6},{6,7},{7,0},{8,9},{9,10},{10,1... | collective-permute-start | bytes 49160 | tf_op jit(solution)/shard_map/ppermute | solution.py:215
  14.9 0.0 copy-start.13
  14.9 0.7 copy-done.13
  15.5 0.6 dynamic_slice.11
  16.7 0.0 collective-permute-done.1.high
  16.8 0.0 copy-start.4
  16.8 0.0 collective-permute-done.low
  16.8 0.0 copy-start.5
  16.8 0.0 copy-done.1
  16.8 0.6 copy-done.4
  17.4 0.0 copy-done.5
  17.4 0.0 copy-start.12
  17.4 1.9 %shard_map.91 = (f32[3,4,2048]{2,1,0:T(4,128)}, f32[3,4,512]{2,1,0:T(4,128)}, f32[3,4,512]{2,1,0:T(4,128)}) custom-call(s32[1]{0:T(128)} %bitcast.2.sel, f32[3,4,2048]{2,1,0:T(4,128)} %copy-done.1, f32[3,4,2048]{2,1,0:T(4,128)} %copy-done.5, f32[3,4,2048]{2,1,0:T(4,128)} %copy-done.4, s32[1,1024]{1,0:T(1,128)} %gs.5), custom_call_target="tpu_custom_call" | custom-call | bytes 1048576 | tf_op jit(solution)/shard_map/pallas_call | solution.py:190
  19.3 0.0 copy-done
  19.3 1.5 %collective-permute-start.2 = (f32[3,4,512]{2,1,0:T(4,128)}, f32[3,4,512]{2,1,0:T(4,128)S(1)}, u32[]{:S(2)}, u32[]{:S(2)}) collective-permute-start(f32[3,4,512]{2,1,0:T(4,128)} %get-tuple-element.16), channel_id=1, source_target_pairs={{0,1},{1,2},{2,3},{3,4},{4,5},{5,6},{6,7},{7,0},{8,9},{9,10},{10,1... | collective-permute-start | bytes 73736 | tf_op jit(solution)/shard_map/ppermute | solution.py:215
  20.8 0.0 copy-start.14
  20.8 3.2 %collective-permute-start.3 = (f32[3,4,512]{2,1,0:T(4,128)}, f32[3,4,512]{2,1,0:T(4,128)S(1)}, u32[]{:S(2)}, u32[]{:S(2)}) collective-permute-start(f32[3,4,512]{2,1,0:T(4,128)} %get-tuple-element.17), channel_id=1, source_target_pairs={{1,0},{2,1},{3,2},{4,3},{5,4},{6,5},{7,6},{0,7},{9,8},{10,9},{11,1... | collective-permute-start | bytes 73736 | tf_op jit(solution)/shard_map/ppermute | solution.py:215
  24.1 0.0 collective-permute-done.4.from_low
  24.1 0.0 copy-start.10
  24.1 0.0 copy-done.12
  24.1 0.6 collective-permute-start.5
  24.6 0.0 copy-done.14
  24.6 0.6 dynamic_slice.9
  26.4 0.0 copy-start.15
  27.1 0.0 copy-done.15
  27.1 0.6 dynamic_slice.10.strength
  27.8 0.2 collective-permute-done.5.from_high
  27.9 0.0 copy-start.11
  27.9 0.0 copy-done.10
  27.9 0.6 copy-done.11
  28.5 10.0 %shard_map.93.gathered = f32[16,8,2,8,128]{4,3,2,1,0:T(8,128)} custom-call(f32[2,4,2048]{2,1,0:T(4,128)} %get-tuple-element.18.par, f32[2,4,512]{2,1,0:T(4,128)} %copy-done.10, f32[2,4,512]{2,1,0:T(4,128)} %copy-done.11, s32[16,2048]{1,0:T(8,128)} %bitcast.11), custom_call_target="tpu_custom_call" | custom-call | flops 16777216 | bytes 1048576 | tf_op jit(solution)/shard_map/pallas_call | solution.py:190
  38.5 0.0 collective-permute-done.7.high
  38.5 0.0 copy-start.2
  38.5 0.0 collective-permute-done.6.low
  38.5 0.0 copy-start.3
  38.6 0.0 collective-permute-done.2.from_low
  38.6 0.0 copy-start.6
  38.6 0.0 collective-permute-done.3.from_high
  38.6 0.0 copy-start.7
  38.6 0.6 copy-done.2
  39.2 0.0 copy-done.3
  39.2 0.0 copy-done.6
  39.2 0.0 copy-done.7
  39.2 15.0 %shard_map.94 = (f32[3,4,2048]{2,1,0:T(4,128)}, f32[3,4,2048]{2,1,0:T(4,128)}, f32[3,4,512]{2,1,0:T(4,128)}, f32[3,4,512]{2,1,0:T(4,128)}) custom-call(s32[1]{0:T(128)} %bitcast.2.sel, f32[1]{0:T(128)} %dynamic_slice.10.strength, f32[3,4,2048]{2,1,0:T(4,128)} %get-tuple-element.15.pos, f32[3,4,512]{2,1,0:T(4,128)} %copy-done.6, f32[3,4,512]{2,1,0:T(4,128)} %copy-done.7, ...), custom_call_target="tpu_custom_call" | custom-call | flops 33554432 | bytes 1048576 | tf_op jit(solution)/shard_map/pallas_call | solution.py:190
  54.2 1.3 %collective-permute-start.8 = (f32[3,4,512]{2,1,0:T(4,128)}, f32[3,4,512]{2,1,0:T(4,128)S(1)}, u32[]{:S(2)}, u32[]{:S(2)}) collective-permute-start(f32[3,4,512]{2,1,0:T(4,128)} %get-tuple-element.22), channel_id=1, source_target_pairs={{0,1},{1,2},{2,3},{3,4},{4,5},{5,6},{6,7},{7,0},{8,9},{9,10},{10,1... | collective-permute-start | bytes 73736 | tf_op jit(solution)/shard_map/ppermute | solution.py:215
  55.5 3.4 %collective-permute-start.9 = (f32[3,4,512]{2,1,0:T(4,128)}, f32[3,4,512]{2,1,0:T(4,128)S(1)}, u32[]{:S(2)}, u32[]{:S(2)}) collective-permute-start(f32[3,4,512]{2,1,0:T(4,128)} %get-tuple-element.23), channel_id=1, source_target_pairs={{1,0},{2,1},{3,2},{4,3},{5,4},{6,5},{7,6},{0,7},{9,8},{10,9},{11,1... | collective-permute-start | bytes 73736 | tf_op jit(solution)/shard_map/ppermute | solution.py:215
  58.9 2.0 %collective-permute-done.8.from_low = f32[3,4,512]{2,1,0:T(4,128)S(1)} collective-permute-done((f32[3,4,512]{2,1,0:T(4,128)}, f32[3,4,512]{2,1,0:T(4,128)S(1)}, u32[]{:S(2)}, u32[]{:S(2)}) %collective-permute-start.8) | collective-permute-done | bytes 24608 | tf_op jit(solution)/shard_map/ppermute | solution.py:215
  60.9 0.0 copy-start.8
  61.0 0.0 collective-permute-done.9.from_high
  61.0 0.0 copy-start.9
  61.0 0.6 copy-done.8
  61.5 0.0 copy-done.9
  61.6 14.7 %shard_map.95 = f32[6,4,2048]{2,1,0:T(4,128)} custom-call(f32[1]{0:T(128)} %dynamic_slice.10.strength, f32[3,4,2048]{2,1,0:T(4,128)} %get-tuple-element.21.pos, f32[3,4,512]{2,1,0:T(4,128)} %copy-done.8, f32[3,4,512]{2,1,0:T(4,128)} %copy-done.9, f32[2,4,2048]{2,1,0:T(4,128)} %get-tuple-element.18.par, f32[16,8,2,8,128]{4,3,2,1,0:T(8,128)} %shard_map.93.gathered, ...), custom_call_target="tpu_custom_call" | custom-call | flops 33554432 | bytes 1048576 | tf_op jit(solution)/shard_map/pallas_call | solution.py:190
Async XLA Ops:
  1.0 15.8 %copy-start.1 = (f32[3,4,2048]{2,1,0:T(4,128)}, f32[3,4,2048]{2,1,0:T(4,128)S(1)}, u32[]{:S(2)}) copy-start(f32[3,4,2048]{2,1,0:T(4,128)S(1)} %get-tuple-element.26.mine) | copy-start | bytes 294916
  1.0 18.4 %copy-start = (f32[3,4,2048]{2,1,0:T(4,128)}, f32[3,4,2048]{2,1,0:T(4,128)S(1)}, u32[]{:S(2)}) copy-start(f32[3,4,2048]{2,1,0:T(4,128)S(1)} %get-tuple-element.25.mine) | copy-start | bytes 294916
  1.0 15.8 %collective-permute-start.1 = (f32[3,4,2048]{2,1,0:T(4,128)S(1)}, f32[3,4,2048]{2,1,0:T(4,128)S(1)}, u32[]{:S(2)}, u32[]{:S(2)}) collective-permute-start(f32[3,4,2048]{2,1,0:T(4,128)S(1)} %get-tuple-element.26.mine), channel_id=1, source_target_pairs={{8,0},{16,8},{24,16},{9,1},{17,9},{25,17},{10,2},{18,10},{26,18},{... | collective-permute-start | bytes 294920 | tf_op jit(solution)/shard_map/ppermute | solution.py:218
  2.3 14.5 %collective-permute-start = (f32[3,4,2048]{2,1,0:T(4,128)S(1)}, f32[3,4,2048]{2,1,0:T(4,128)S(1)}, u32[]{:S(2)}, u32[]{:S(2)}) collective-permute-start(f32[3,4,2048]{2,1,0:T(4,128)S(1)} %get-tuple-element.26.mine), channel_id=1, source_target_pairs={{0,8},{8,16},{16,24},{1,9},{9,17},{17,25},{2,10},{10,18},{18,26},{... | collective-permute-start | bytes 294920 | tf_op jit(solution)/shard_map/ppermute | solution.py:218
  5.3 33.2 %collective-permute-start.7 = (f32[3,4,2048]{2,1,0:T(4,128)S(1)}, f32[3,4,2048]{2,1,0:T(4,128)S(1)}, u32[]{:S(2)}, u32[]{:S(2)}) collective-permute-start(f32[3,4,2048]{2,1,0:T(4,128)S(1)} %get-tuple-element.25.mine), channel_id=1, source_target_pairs={{8,0},{16,8},{24,16},{9,1},{17,9},{25,17},{10,2},{18,10},{26,18},{... | collective-permute-start | bytes 294920 | tf_op jit(solution)/shard_map/ppermute | solution.py:219
  6.6 31.9 %collective-permute-start.6 = (f32[3,4,2048]{2,1,0:T(4,128)S(1)}, f32[3,4,2048]{2,1,0:T(4,128)S(1)}, u32[]{:S(2)}, u32[]{:S(2)}) collective-permute-start(f32[3,4,2048]{2,1,0:T(4,128)S(1)} %get-tuple-element.25.mine), channel_id=1, source_target_pairs={{0,8},{8,16},{16,24},{1,9},{9,17},{17,25},{2,10},{10,18},{18,26},{... | collective-permute-start | bytes 294920 | tf_op jit(solution)/shard_map/ppermute | solution.py:219
  13.4 10.7 %collective-permute-start.4 = (f32[2,4,512]{2,1,0:T(4,128)}, f32[2,4,512]{2,1,0:T(4,128)S(1)}, u32[]{:S(2)}, u32[]{:S(2)}) collective-permute-start(f32[2,4,512]{2,1,0:T(4,128)} %get-tuple-element.19), channel_id=1, source_target_pairs={{0,1},{1,2},{2,3},{3,4},{4,5},{5,6},{6,7},{7,0},{8,9},{9,10},{10,1... | collective-permute-start | bytes 49160 | tf_op jit(solution)/shard_map/ppermute | solution.py:215
  14.9 0.7 copy-start.13
  16.8 0.6 copy-start.4
  16.8 0.7 copy-start.5
  17.4 6.6 %copy-start.12 = (f32[2,4,512]{2,1,0:T(4,128)S(1)}, f32[2,4,512]{2,1,0:T(4,128)}, u32[]{:S(2)}) copy-start(f32[2,4,512]{2,1,0:T(4,128)} %get-tuple-element.20) | copy-start | bytes 49156
  19.3 19.2 %collective-permute-start.2 = (f32[3,4,512]{2,1,0:T(4,128)}, f32[3,4,512]{2,1,0:T(4,128)S(1)}, u32[]{:S(2)}, u32[]{:S(2)}) collective-permute-start(f32[3,4,512]{2,1,0:T(4,128)} %get-tuple-element.16), channel_id=1, source_target_pairs={{0,1},{1,2},{2,3},{3,4},{4,5},{5,6},{6,7},{7,0},{8,9},{9,10},{10,1... | collective-permute-start | bytes 73736 | tf_op jit(solution)/shard_map/ppermute | solution.py:215
  20.8 3.8 %copy-start.14 = (s32[4]{0:T(128)S(1)}, s32[4]{0:T(128)}, u32[]{:S(2)}) copy-start(s32[4]{0:T(128)} %param.16) | copy-start | bytes 52
  20.8 17.7 %collective-permute-start.3 = (f32[3,4,512]{2,1,0:T(4,128)}, f32[3,4,512]{2,1,0:T(4,128)S(1)}, u32[]{:S(2)}, u32[]{:S(2)}) collective-permute-start(f32[3,4,512]{2,1,0:T(4,128)} %get-tuple-element.17), channel_id=1, source_target_pairs={{1,0},{2,1},{3,2},{4,3},{5,4},{6,5},{7,6},{0,7},{9,8},{10,9},{11,1... | collective-permute-start | bytes 73736 | tf_op jit(solution)/shard_map/ppermute | solution.py:215
  24.1 3.9 %copy-start.10 = (f32[2,4,512]{2,1,0:T(4,128)}, f32[2,4,512]{2,1,0:T(4,128)S(1)}, u32[]{:S(2)}) copy-start(f32[2,4,512]{2,1,0:T(4,128)S(1)} %collective-permute-done.4.from_low) | copy-start | bytes 49156
  24.1 3.9 %collective-permute-start.5 = (f32[2,4,512]{2,1,0:T(4,128)S(1)}, f32[2,4,512]{2,1,0:T(4,128)S(1)}, u32[]{:S(2)}, u32[]{:S(2)}) collective-permute-start(f32[2,4,512]{2,1,0:T(4,128)S(1)} %copy-done.12), channel_id=1, source_target_pairs={{1,0},{2,1},{3,2},{4,3},{5,4},{6,5},{7,6},{0,7},{9,8},{10,9},{11,1... | collective-permute-start | bytes 49160 | tf_op jit(solution)/shard_map/ppermute | solution.py:215
  26.4 0.7 copy-start.15
  27.9 0.6 copy-start.11
  38.5 0.6 copy-start.2
  38.5 0.7 copy-start.3
  38.6 0.6 copy-start.6
  38.6 0.6 copy-start.7
  54.2 6.7 %collective-permute-start.8 = (f32[3,4,512]{2,1,0:T(4,128)}, f32[3,4,512]{2,1,0:T(4,128)S(1)}, u32[]{:S(2)}, u32[]{:S(2)}) collective-permute-start(f32[3,4,512]{2,1,0:T(4,128)} %get-tuple-element.22), channel_id=1, source_target_pairs={{0,1},{1,2},{2,3},{3,4},{4,5},{5,6},{6,7},{7,0},{8,9},{9,10},{10,1... | collective-permute-start | bytes 73736 | tf_op jit(solution)/shard_map/ppermute | solution.py:215
  55.5 5.4 %collective-permute-start.9 = (f32[3,4,512]{2,1,0:T(4,128)}, f32[3,4,512]{2,1,0:T(4,128)S(1)}, u32[]{:S(2)}, u32[]{:S(2)}) collective-permute-start(f32[3,4,512]{2,1,0:T(4,128)} %get-tuple-element.23), channel_id=1, source_target_pairs={{1,0},{2,1},{3,2},{4,3},{5,4},{6,5},{7,6},{0,7},{9,8},{10,9},{11,1... | collective-permute-start | bytes 73736 | tf_op jit(solution)/shard_map/ppermute | solution.py:215
  60.9 0.6 copy-start.8
  61.0 0.6 copy-start.9

commit v2 on v0

v2 whole, which is shorter than its diff:
```python
import jax
import jax.numpy as jnp
from jax import lax
from jax.experimental import pallas as pl
from jax.experimental.pallas import tpu as pltpu
from jax.sharding import PartitionSpec as P

STEPS = 2
LANES = 128

time_step = 0.2
softening = 0.5

VMEM = pl.BlockSpec(memory_space=pltpu.VMEM)
SMEM = pl.BlockSpec(memory_space=pltpu.SMEM)
MESH = pl.DeviceIdType.MESH
f32 = jnp.float32
i32 = jnp.int32

POS = float((1 << 20) - 2)
LOW = (1 << 11) - 1
Q_STEPS = 8191.0
E_STEPS = 32767.0


def upper_half():
    return lax.broadcasted_iota(i32, (8, LANES), 0) >= 4


def row(values):
    return jnp.broadcast_to(values, (8, LANES))


def twice(tile):
    return jnp.concatenate([tile, tile], 0)


def lookup(tabs, first, count, low, high):
    bits = max(count - 1, 0).bit_length()
    masks = [(high & (1 << b)) != 0 for b in range(bits)]

    def find(tab, bit, start):
        if bit < 0:
            return jnp.take_along_axis(tab[first + start], low, axis=1)
        lower = find(tab, bit - 1, start)
        if start + (1 << bit) >= count:
            return lower
        return jnp.where(masks[bit], find(tab, bit - 1, start + (1 << bit)), lower)

    return [find(tab, bits - 1, 0) for tab in tabs]


def find_in_pool(tabs, own, tiles, index):
    low, high = index & (LANES - 1), index >> 7
    here = lookup(tabs, 0, own, low, high)
    there = lookup(tabs, own, tiles - own, low, high - own)
    return [jnp.where(high < own, a, b) for a, b in zip(here, there)]


def pair_index(near, pair, base):
    return jnp.where(
        upper_half(),
        row(near[2 * pair + 1 : 2 * pair + 2, pl.ds(base, LANES)]),
        row(near[2 * pair : 2 * pair + 1, pl.ds(base, LANES)]),
    )


def fill_exact(tab, block):
    for k in range(block.shape[1] // LANES):
        tab[k] = twice(block[:, k * LANES : (k + 1) * LANES])


def gather_ghosts(tab, comps, own, gs, out_first, out_last):
    width = out_first.shape[2]
    up = upper_half()
    for g in range(width // LANES):
        index = jnp.where(
            up,
            row(gs[:, width + g * LANES : width + (g + 1) * LANES]),
            row(gs[:, g * LANES : (g + 1) * LANES]),
        )
        found = lookup([tab.at[c] for c in range(comps)], 0, own, index & (LANES - 1), index >> 7)
        for c in range(comps):
            out_first[c, :, g * LANES : (g + 1) * LANES] = found[c][:4]
            out_last[c, :, g * LANES : (g + 1) * LANES] = found[c][4:]


def pack_params(tab, first, par):
    for k in range(par.shape[2] // LANES):
        cut = slice(k * LANES, (k + 1) * LANES)
        q = (par[0, :, cut] * Q_STEPS + 32768.5).astype(i32) - 32768
        e = (par[1, :, cut] * E_STEPS + 0.5).astype(i32)
        tab[first + k] = twice((q << 16) | e)


def largest(blocks):
    top = None
    for block in blocks:
        for c in range(3):
            here = jnp.max(jnp.abs(block[c]), axis=0, keepdims=True)
            here = jnp.max(here, axis=1, keepdims=True)
            top = here if top is None else jnp.maximum(top, here)
    return jnp.maximum(top, 1e-30)


def pack_positions(tabs, first, pos, top):
    factor = POS / top
    for k in range(pos.shape[2] // LANES):
        cut = slice(k * LANES, (k + 1) * LANES)
        x = (pos[0, :, cut] * factor + (1048576.5)).astype(i32) - 1048576
        y = (pos[1, :, cut] * factor + (1048576.5)).astype(i32) - 1048576
        z = (pos[2, :, cut] * factor * 2.0 + (2097152.5)).astype(i32)
        tabs[0][first + k] = twice((x << 11) | (z >> 11))
        tabs[1][first + k] = twice((y << 11) | (z & LOW))


def unpack_positions(words, unit):
    x = (words[0] >> 11).astype(f32) * unit
    y = (words[1] >> 11).astype(f32) * unit
    z = (((words[0] & LOW) << 11) | (words[1] & LOW)).astype(f32)
    return x, y, (z - 2097152.0) * (0.5 * unit)


def forces(pos, par, base, found, charges, depths):
    lanes = pl.ds(base, LANES)
    force = [[None] * 4 for _ in range(3)]
    for pair in range(len(charges)):
        there = found(pair)
        charge, depth = charges[pair], depths[pair]
        for i in range(4):
            offset = [row(pos[c, i : i + 1, lanes]) - there[c] for c in range(3)]
            square = offset[0] * offset[0] + offset[1] * offset[1] + offset[2] * offset[2]
            root = lax.rsqrt(square + softening)
            w = root * root
            qq = row(par[0, i : i + 1, lanes]) * charge
            ee = row(par[1, i : i + 1, lanes]) * depth
            weight = w * (qq * root + ee * (w * w - w))
            for c in range(3):
                term = weight * offset[c]
                force[c][i] = term if pair == 0 else force[c][i] + term
    return [
        jnp.concatenate([jnp.sum(force[c][i], axis=0, keepdims=True) for i in range(4)], 0)
        for c in range(3)
    ]


def kernel(
    partner, scale_order, coupling, phase, charges, lj, fill, near, gs, out,
    from_low, from_high, par, par_first, par_last, par_low, par_high,
    pos_first, pos_last, pos_low, pos_high, pos, pos_next, vel,
    exact, packed_par, packed_pos, gathered, part, send_sem, recv_sem,
):
    total, width = phase.shape[2], gs.shape[1] // 2
    own, ghost = total // LANES, width // LANES
    tiles = own + 2 * ghost
    pairs = near.shape[0] // 2
    level, levels = lax.axis_index("rep"), lax.axis_size("rep")
    place, places = lax.axis_index("space"), lax.axis_size("space")
    has_low, has_high = level > 0, level < levels - 1
    above, below = lax.rem(place + 1, places), lax.rem(place + places - 1, places)

    barrier = pltpu.get_barrier_semaphore()

    def greet(device):
        pl.semaphore_signal(barrier, inc=1, device_id=device, device_id_type=MESH)

    greet({"space": above})
    greet({"space": below})

    @pl.when(has_low)
    def _():
        greet({"rep": level - 1})

    @pl.when(has_high)
    def _():
        greet({"rep": level + 1})

    pl.semaphore_wait(barrier, 2 + jnp.where(has_low, 1, 0) + jnp.where(has_high, 1, 0))

    def remote(src, dst, number, device):
        return pltpu.make_async_remote_copy(
            src_ref=src, dst_ref=dst, send_sem=send_sem.at[number], recv_sem=recv_sem.at[number],
            device_id=device, device_id_type=MESH,
        )

    halves = (pl.ds(0, 3), pl.ds(3, 3))
    rising = [remote(phase.at[h], from_low.at[h], n, {"rep": level + 1}) for n, h in enumerate(halves)]
    falling = [remote(phase.at[h], from_high.at[h], 2 + n, {"rep": level - 1}) for n, h in enumerate(halves)]

    for n in range(2):

        @pl.when(has_high)
        def _():
            rising[n].start()

        @pl.when(has_low)
        def _():
            falling[n].start()

    def swap_arrived(n):
        @pl.when(has_low)
        def _():
            rising[n].wait_recv()

        @pl.when(has_high)
        def _():
            falling[n].wait_recv()

    def ring(first, last, low, high, number):
        return [remote(last, low, number, {"space": above}), remote(first, high, number + 1, {"space": below})]

    slot = lax.broadcasted_iota(i32, (4, total), 0)
    present = (slot < fill[...]).astype(f32)
    par[0] = charges[...] * present
    par[1] = lj[...] * present
    for c in range(2):
        fill_exact(exact.at[c], par[c])
    gather_ghosts(exact, 2, own, gs, par_first, par_last)
    par_ring = ring(par_first, par_last, par_low, par_high, 4)
    for copy in par_ring:
        copy.start()
    pack_params(packed_par, 0, par)

    moved = partner[level] - level

    def swapped(c, lanes):
        return jnp.where(
            moved == 0, phase[c, :, lanes],
            jnp.where(moved < 0, from_low[c, :, lanes], from_high[c, :, lanes]),
        )

    swap_arrived(0)
    for c in range(3):
        block = swapped(c, pl.ds(0, total))
        pos[c] = block
        fill_exact(exact.at[c], block)
    gather_ghosts(exact, 3, own, gs, pos_first.at[0], pos_last.at[0])
    pos_rings = [
        ring(pos_first.at[n], pos_last.at[n], pos_low.at[n], pos_high.at[n], 6 + 2 * n) for n in range(2)
    ]
    for copy in pos_rings[0]:
        copy.start()
    tabs = [packed_pos.at[0], packed_pos.at[1]]
    top_own = largest([pos])
    pack_positions(tabs, 0, pos, top_own)
    unit_own = top_own * (1.0 / POS)

    for copy in par_ring:
        copy.wait_recv()
    pack_params(packed_par, own, par_low)
    pack_params(packed_par, own + ghost, par_high)
    strength = coupling[scale_order[level]] * (1.0 / Q_STEPS)

    def gather_params(group, carry):
        base = pl.multiple_of(group * LANES, LANES)
        for pair in range(pairs):
            (word,) = find_in_pool([packed_par], own, tiles, pair_index(near, pair, base))
            gathered[group, pair, 0] = (word >> 16).astype(f32) * strength
            gathered[group, pair, 1] = (word & 65535).astype(f32) * (1.0 / E_STEPS)
        return carry

    lax.fori_loop(0, own, gather_params, 0)

    def ghosts_arrived(n):
        for copy in pos_rings[n]:
            copy.wait_recv()
        low, high = pos_low.at[n], pos_high.at[n]
        top = largest([low, high])
        pack_positions(tabs, own, low, top)
        pack_positions(tabs, own + ghost, high, top)
        return top * (1.0 / POS)

    def params_of(group):
        return (
            [gathered[group, pair, 0] for pair in range(pairs)],
            [gathered[group, pair, 1] for pair in range(pairs)],
        )

    swap_arrived(1)
    unit_ghost = ghosts_arrived(0)

    def first_step(group, carry):
        base = pl.multiple_of(group * LANES, LANES)
        lanes = pl.ds(base, LANES)

        def found(pair):
            index = pair_index(near, pair, base)
            words = find_in_pool(tabs, own, tiles, index)
            return unpack_positions(words, jnp.where(index < total, unit_own, unit_ghost))

        force = forces(pos, par, base, found, *params_of(group))
        for c in range(3):
            v = swapped(3 + c, lanes) + time_step * force[c]
            vel[c, :, lanes] = v
            pos_next[c, :, lanes] = pos[c, :, lanes] + time_step * v
        return carry

    lax.fori_loop(0, own, first_step, 0)

    for c in range(3):
        fill_exact(exact.at[c], pos_next[c])
    gather_ghosts(exact, 3, own, gs, pos_first.at[1], pos_last.at[1])
    for copy in pos_rings[1]:
        copy.start()
    top_own = largest([pos_next])
    pack_positions(tabs, 0, pos_next, top_own)
    unit_own_next = top_own * (1.0 / POS)

    def own_part(group, carry):
        base = pl.multiple_of(group * LANES, LANES)
        for pair in range(pairs):
            index = pair_index(near, pair, base)
            words = lookup(tabs, 0, own, index & (LANES - 1), index >> 7)
            part[group, pair, 0] = words[0]
            part[group, pair, 1] = words[1]
        return carry

    lax.fori_loop(0, own, own_part, 0)
    unit_ghost_next = ghosts_arrived(1)

    def second_step(group, carry):
        base = pl.multiple_of(group * LANES, LANES)
        lanes = pl.ds(base, LANES)

        def found(pair):
            index = pair_index(near, pair, base)
            words = lookup(tabs, own, tiles - own, index & (LANES - 1), (index >> 7) - own)
            here = index < total
            words = [jnp.where(here, part[group, pair, n], words[n]) for n in range(2)]
            return unpack_positions(words, jnp.where(here, unit_own_next, unit_ghost_next))

        force = forces(pos_next, par, base, found, *params_of(group))
        for c in range(3):
            v = vel[c, :, lanes] + time_step * force[c]
            out[3 + c, :, lanes] = v
            out[c, :, lanes] = pos_next[c, :, lanes] + time_step * v
        return carry

    lax.fori_loop(0, own, second_step, 0)

    for copy in par_ring + pos_rings[0] + pos_rings[1]:
        copy.wait_send()
    for n in range(2):

        @pl.when(has_high)
        def _():
            rising[n].wait_send()

        @pl.when(has_low)
        def _():
            falling[n].wait_send()


def on_device(
    phase_space, charges, lj_depth, cluster_fill, neighbours, ghost_send, partner, scale_order, coupling
):
    phase = phase_space[0]
    rows, slots, total = phase.shape
    width = ghost_send.shape[1] // 2
    own = total // LANES
    tiles = own + 2 * (width // LANES)
    pairs = neighbours.shape[1] // 2
    out = pl.pallas_call(
        kernel,
        out_shape=jax.ShapeDtypeStruct(phase.shape, f32),
        in_specs=[SMEM] * 3 + [VMEM] * 6,
        out_specs=VMEM,
        scratch_shapes=[
            pltpu.VMEM((rows, slots, total), f32),
            pltpu.VMEM((rows, slots, total), f32),
            pltpu.VMEM((2, slots, total), f32),
        ]
        + [pltpu.VMEM((2, slots, width), f32)] * 4
        + [pltpu.VMEM((2, 3, slots, width), f32)] * 4
        + [pltpu.VMEM((3, slots, total), f32)] * 3
        + [
            pltpu.VMEM((3, own, 8, LANES), f32),
            pltpu.VMEM((tiles, 8, LANES), i32),
            pltpu.VMEM((2, tiles, 8, LANES), i32),
            pltpu.VMEM((own, pairs, 2, 8, LANES), f32),
            pltpu.VMEM((own, pairs, 2, 8, LANES), i32),
            pltpu.SemaphoreType.DMA((10,)),
            pltpu.SemaphoreType.DMA((10,)),
        ],
        compiler_params=pltpu.CompilerParams(collective_id=0, has_side_effects=True),
    )(partner, scale_order, coupling, phase, charges[0], lj_depth[0], cluster_fill, neighbours[0], ghost_send)
    return out[None]


def solution(mesh):
    return jax.shard_map(
        on_device,
        mesh=mesh,
        in_specs=(
            P("rep", None, None, "space"),
            P("rep", None, "space"),
            P("rep", None, "space"),
            P("rep", "space"),
            P("rep", None, "space"),
            P("rep", "space"),
            P(),
            P(),
            P(),
        ),
        out_specs=P("rep", None, None, "space"),
        check_vma=False,
    )
```

time: 1290 us -> 38.8 us (0.03)
  the two profiles are of different devices: /device:TPU:0 before, /device:TPU:1 now
where the time goes in v2:
time: 38.8 us; the launch traced here: 38.7 us
  Pallas kernels  37 us (95%)
  local copies, waits for them, and re-layouts  1.62 us (4%)
    pallas_call x1, Pallas kernels, on_device(): pl.pallas_call(kernel, out_shape=jax.ShapeDtypeStruct(phase.shape, f32),...  37 us
    unnamed x1, local copies, waits for them, and re-layouts  1.62 us

profile of v2, /device:TPU:1, one launch (start us, length us, event | category | flops | bytes accessed | tf_op | source)
XLA Modules:
  0.0 38.7 jit_solution(10050067961613532307)
XLA Ops:
  0.0 37.0 %shard_map.91 = f32[6,4,2048]{2,1,0:T(4,128)} custom-call(s32[4]{0:T(128)} %partner.1, s32[4]{0:T(128)} %scale_order.1, f32[4]{0:T(128)} %coupling.1, f32[6,4,2048]{2,1,0:T(4,128)} %bitcast.6, f32[4,2048]{1,0:T(4,128)} %bitcast.8, f32[4,2048]{1,0:T(4,128)} %bitcast.9, s32[1,2048]{1,0:T(1,128)} %fill.1, s32[16,2048]{1,0:T(8,128)} %bitcast.7, s32[1,1024]{1,0:T(1,128)} %gs.1), custom_call_target="tpu_custom_call" | custom-call | tf_op jit(solution)/shard_map/pallas_call | solution.py:363
  37.0 1.6 %copy.11 = f32[1,6,4,2048]{3,2,1,0:T(4,128)} copy(f32[1,6,4,2048]{3,2,1,0:T(4,128)} %bitcast.5) | data formatting | bytes 393216

commit v3 on v2

--- a/solution.py
+++ b/solution.py
@@ -220,6 +220,30 @@
     for copy in par_ring:
         copy.start()
     pack_params(packed_par, 0, par)
+    early, ahead = own // 4, own * 5 // 8
+
+    def each_group(start, stop, body):
+        def step(group, carry):
+            body(group, pl.multiple_of(group * LANES, LANES))
+            return carry
+
+        lax.fori_loop(start, stop, step, 0, unroll=2)
+
+    def look_ahead(tabs):
+        def body(group, base):
+            for pair in range(pairs):
+                index = pair_index(near, pair, base)
+                words = lookup(tabs, 0, own, index & (LANES - 1), index >> 7)
+                for n, word in enumerate(words):
+                    part[group, pair, n] = word
+
+        return body
+
+    def find_rest(tabs, group, pair, index):
+        words = lookup(tabs, own, tiles - own, index & (LANES - 1), (index >> 7) - own)
+        return [jnp.where(index < total, part[group, pair, n], word) for n, word in enumerate(words)]
+
+    each_group(0, early, look_ahead([packed_par]))
 
     moved = partner[level] - level
 
@@ -251,15 +275,20 @@
     pack_params(packed_par, own + ghost, par_high)
     strength = coupling[scale_order[level]] * (1.0 / Q_STEPS)
 
-    def gather_params(group, carry):
-        base = pl.multiple_of(group * LANES, LANES)
+    def keep_params(group, pair, word):
+        gathered[group, pair, 0] = (word >> 16).astype(f32) * strength
+        gathered[group, pair, 1] = (word & 65535).astype(f32) * (1.0 / E_STEPS)
+
+    def finish_params(group, base):
         for pair in range(pairs):
-            (word,) = find_in_pool([packed_par], own, tiles, pair_index(near, pair, base))
-            gathered[group, pair, 0] = (word >> 16).astype(f32) * strength
-            gathered[group, pair, 1] = (word & 65535).astype(f32) * (1.0 / E_STEPS)
-        return carry
-
-    lax.fori_loop(0, own, gather_params, 0)
+            keep_params(group, pair, find_rest([packed_par], group, pair, pair_index(near, pair, base))[0])
+
+    def gather_params(group, base):
+        for pair in range(pairs):
+            keep_params(group, pair, find_in_pool([packed_par], own, tiles, pair_index(near, pair, base))[0])
+
+    each_group(0, early, finish_params)
+    each_group(early, own, gather_params)
 
     def ghosts_arrived(n):
         for copy in pos_rings[n]:
@@ -279,8 +308,7 @@
     swap_arrived(1)
     unit_ghost = ghosts_arrived(0)
 
-    def first_step(group, carry):
-        base = pl.multiple_of(group * LANES, LANES)
+    def first_step(group, base):
         lanes = pl.ds(base, LANES)
 
         def found(pair):
@@ -293,9 +321,8 @@
             v = swapped(3 + c, lanes) + time_step * force[c]
             vel[c, :, lanes] = v
             pos_next[c, :, lanes] = pos[c, :, lanes] + time_step * v
-        return carry
-
-    lax.fori_loop(0, own, first_step, 0)
+
+    each_group(0, own, first_step)
 
     for c in range(3):
         fill_exact(exact.at[c], pos_next[c])
@@ -306,37 +333,31 @@
     pack_positions(tabs, 0, pos_next, top_own)
     unit_own_next = top_own * (1.0 / POS)
 
-    def own_part(group, carry):
-        base = pl.multiple_of(group * LANES, LANES)
-        for pair in range(pairs):
-            index = pair_index(near, pair, base)
-            words = lookup(tabs, 0, own, index & (LANES - 1), index >> 7)
-            part[group, pair, 0] = words[0]
-            part[group, pair, 1] = words[1]
-        return carry
-
-    lax.fori_loop(0, own, own_part, 0)
+    each_group(0, ahead, look_ahead(tabs))
     unit_ghost_next = ghosts_arrived(1)
 
-    def second_step(group, carry):
-        base = pl.multiple_of(group * LANES, LANES)
-        lanes = pl.ds(base, LANES)
-
-        def found(pair):
-            index = pair_index(near, pair, base)
-            words = lookup(tabs, own, tiles - own, index & (LANES - 1), (index >> 7) - own)
-            here = index < total
-            words = [jnp.where(here, part[group, pair, n], words[n]) for n in range(2)]
-            return unpack_positions(words, jnp.where(here, unit_own_next, unit_ghost_next))
-
-        force = forces(pos_next, par, base, found, *params_of(group))
-        for c in range(3):
-            v = vel[c, :, lanes] + time_step * force[c]
-            out[3 + c, :, lanes] = v
-            out[c, :, lanes] = pos_next[c, :, lanes] + time_step * v
-        return carry
-
-    lax.fori_loop(0, own, second_step, 0)
+    def second_step(looked_up):
+        def body(group, base):
+            lanes = pl.ds(base, LANES)
+
+            def found(pair):
+                index = pair_index(near, pair, base)
+                if looked_up:
+                    words = find_rest(tabs, group, pair, index)
+                else:
+                    words = find_in_pool(tabs, own, tiles, index)
+                return unpack_positions(words, jnp.where(index < total, unit_own_next, unit_ghost_next))
+
+            force = forces(pos_next, par, base, found, *params_of(group))
+            for c in range(3):
+                v = vel[c, :, lanes] + time_step * force[c]
+                out[3 + c, :, lanes] = v
+                out[c, :, lanes] = pos_next[c, :, lanes] + time_step * v
+
+        return body
+
+    each_group(0, ahead, second_step(True))
+    each_group(ahead, own, second_step(False))
 
     for copy in par_ring + pos_rings[0] + pos_rings[1]:
         copy.wait_send()

time: 38.8 us -> 35.8 us (0.923)
  the two profiles are of different devices: /device:TPU:1 before, /device:TPU:0 now
where the time goes in v3:
time: 35.8 us; the launch traced here: 35.7 us
  Pallas kernels  34.1 us (95%)
  local copies, waits for them, and re-layouts  1.62 us (5%)
    pallas_call x1, Pallas kernels, on_device(): pl.pallas_call(kernel, out_shape=jax.ShapeDtypeStruct(phase.shape, f32),...  34.1 us
    unnamed x1, local copies, waits for them, and re-layouts  1.62 us

profile of v3, /device:TPU:0, one launch (start us, length us, event | category | flops | bytes accessed | tf_op | source)
XLA Modules:
  0.0 35.7 jit_solution(16639998409211850203)
XLA Ops:
  0.0 34.1 %shard_map.91 = f32[6,4,2048]{2,1,0:T(4,128)} custom-call(s32[4]{0:T(128)} %partner.1, s32[4]{0:T(128)} %scale_order.1, f32[4]{0:T(128)} %coupling.1, f32[6,4,2048]{2,1,0:T(4,128)} %bitcast.6, f32[4,2048]{1,0:T(4,128)} %bitcast.8, f32[4,2048]{1,0:T(4,128)} %bitcast.9, s32[1,2048]{1,0:T(1,128)} %fill.1, s32[16,2048]{1,0:T(8,128)} %bitcast.7, s32[1,1024]{1,0:T(1,128)} %gs.1), custom_call_target="tpu_custom_call" | custom-call | tf_op jit(solution)/shard_map/pallas_call | solution.py:384
  34.1 1.6 %copy.11 = f32[1,6,4,2048]{3,2,1,0:T(4,128)} copy(f32[1,6,4,2048]{3,2,1,0:T(4,128)} %bitcast.5) | data formatting | bytes 393216
